TPU v7x, 256 devices: a whole 4x4x8 slice. The times are simulated.
256 devices in a mesh: slot: 8 (over y_lo, x), feat: 32 (over y_hi, z, core).
Axes of the slice: x: 4, y: 4 (y_hi: 2, y_lo: 2; y = y_hi * 2 + y_lo), z: 8, core: 2. Of those that a mesh axis runs over, the one named last changes fastest.
Arguments:
- acts_in: bfloat16 [3, 256, 2304], P(None, None, 'slot'), may hold values from -6 to 6
- acts_out: bfloat16 [3, 256, 2304], P(None, None, 'slot'), may hold values from -6 to 6
- enc_weight: bfloat16 [3, 2304, 16384], P(None, 'slot', 'feat'), may hold values from -0.125 to 0.125
- enc_bias: float32 [3, 16384], P(None, 'feat'), may hold values from -3 to 3
- dec_weight: bfloat16 [6, 16384, 2304], P(None, 'feat', 'slot'), may hold values from -0.046875 to 0.046875
- dec_bias: float32 [3, 2304], P(None, 'slot'), may hold values from -3 to 3
Outputs:
- enc_grad: float32 [3, 2304, 16384], P(None, 'slot', 'feat')
- enc_bias_grad: float32 [3, 16384], P(None, 'feat')
- dec_grad: float32 [6, 16384, 2304], P(None, 'feat', 'slot')
- mse: float32 [], replicated
All inputs are finite; a program needn't handle non-finite values.
Results may differ from a plain program's by a relative error of at most 0.0095.
Values may be sent and summed in bfloat16 or wider, within the bound.
No kernel may reach another device: no remote copies, remote signals or barrier semaphores. Data moves between devices by JAX's collectives and lax.ppermute only.
A program may use at most 64 MiB of HBM per device.

v0:
```python
import functools
import jax
import jax.numpy as jnp
from jax import lax
from jax.sharding import Mesh
from jax.sharding import PartitionSpec as P

D = 2304
SLOT = ("slot_0", "slot_1")
FEAT = ("feat_0", "feat_1", "feat_2")
SLOT_FEAT = ("slot_0", "slot_1", "feat_0", "feat_1", "feat_2")


def cut_along(x, dim, devices):
    before, after = (x.shape[:dim], x.shape[dim + 1 :])
    return jnp.moveaxis(x.reshape(*before, devices, -1, *after), dim, 0)


def sum_at_owner(x, axis, dim):
    tiles = cut_along(x, dim, lax.axis_size(axis))
    arrived = lax.all_to_all(tiles, axis, split_axis=0, concat_axis=0, tiled=True)
    return arrived.sum(axis=0)


def over_axes(x, axes):
    return functools.reduce(lax.psum, axes, x)


def sent_to_all(x, axis):
    devices = lax.axis_size(axis)
    return lax.all_to_all(jnp.broadcast_to(x[None], (devices, *x.shape)), axis, 0, 0, tiled=True)


def joined_along(tiles, dim):
    dims = list(tiles.shape[1:])
    dims[dim] *= tiles.shape[0]
    return jnp.moveaxis(tiles, 0, dim).reshape(dims)


def collect(x, axis, dim):
    tiles = sent_to_all(x, axis)
    return joined_along(tiles, dim)


def activate(preact):
    return (
        jnp.maximum(preact, 0.0).astype(jnp.bfloat16),
        jnp.where(preact > 0, 1.0, 0.0).astype(jnp.bfloat16),
    )


def local(acts_in, acts_out, enc_weight, enc_bias, dec_weight, dec_bias):
    layers = acts_in.shape[0]
    tokens = acts_in.shape[1]
    width_dev = acts_in.shape[2]
    feature_dev = enc_weight.shape[2]
    pair_list = [(a, b) for a in range(layers) for b in range(a, layers)]

    def encode_rows():
        pieces = [
            jnp.dot(acts_in[a], enc_weight[a], preferred_element_type=jnp.float32)
            for a in range(layers)
        ]
        return jnp.concatenate(pieces, axis=1)

    bias_row = enc_bias.reshape(1, layers * feature_dev)
    preact = lax.psum(encode_rows(), SLOT) + bias_row
    features, slopes = activate(preact)
    target = (
        jnp.transpose(acts_out, (1, 0, 2)).reshape(tokens, layers * width_dev).astype(jnp.float32)
    )
    dec_row = dec_bias.reshape(1, layers * width_dev)
    portion = tokens // lax.axis_size(FEAT)
    row_block = features
    pieces = []
    for decode_b in range(layers):
        summed = jnp.zeros((portion * lax.axis_size(FEAT), width_dev), jnp.float32)
        for decode_a in range(decode_b + 1):
            pair_num = pair_list.index((decode_a, decode_b))
            summed = summed + jnp.dot(
                row_block[:, decode_a * feature_dev : (decode_a + 1) * feature_dev],
                dec_weight[pair_num],
                preferred_element_type=jnp.float32,
            )
        pieces.append(summed)
    rebuilt = sum_at_owner(jnp.concatenate(pieces, axis=1), FEAT, 0)
    offset = lax.axis_index(FEAT) * portion
    error_full = rebuilt + dec_row - lax.dynamic_slice_in_dim(target, offset, portion, 0)
    squared = over_axes(jnp.sum(error_full * error_full), SLOT_FEAT)
    error_half = collect(error_full.astype(jnp.bfloat16), FEAT, 0)
    mse = squared / (layers * tokens * D)
    dec_grads = []
    for a, b in pair_list:
        dec_grads.append(
            lax.dot_general(
                features[:, a * feature_dev : (a + 1) * feature_dev],
                error_half[:, b * width_dev : (b + 1) * width_dev],
                (((0,), (0,)), ((), ())),
                preferred_element_type=jnp.float32,
            )
        )
    row_block = error_half
    partials = []
    for upstream_a in range(layers):
        summed = jnp.zeros((tokens, feature_dev), jnp.float32)
        for b in range(upstream_a, layers):
            pair_num = pair_list.index((upstream_a, b))
            summed = summed + lax.dot_general(
                row_block[:, b * width_dev : (b + 1) * width_dev],
                dec_weight[pair_num],
                (((1,), (1,)), ((), ())),
                preferred_element_type=jnp.float32,
            )
        partials.append(summed)
    upstream = lax.psum(jnp.concatenate(partials, axis=1), SLOT)
    delta = upstream * slopes.astype(jnp.float32)
    bias_grad = jnp.sum(delta, axis=0).reshape(layers, feature_dev)
    delta_half = delta.astype(jnp.bfloat16)
    enc_grads = []
    for a in range(layers):
        enc_grads.append(
            lax.dot_general(
                acts_in[a],
                delta_half[:, a * feature_dev : (a + 1) * feature_dev],
                (((0,), (0,)), ((), ())),
                preferred_element_type=jnp.float32,
            )
        )
    return (jnp.stack(enc_grads), bias_grad, jnp.stack(dec_grads), mse)


def solution(mesh):
    split = Mesh(
        mesh.devices.reshape(2, 4, 2, 8, 2), ("slot_0", "slot_1", "feat_0", "feat_1", "feat_2")
    )
    in_specs = (
        P(None, None, SLOT),
        P(None, None, SLOT),
        P(None, SLOT, FEAT),
        P(None, FEAT),
        P(None, FEAT, SLOT),
        P(None, SLOT),
    )
    out_specs = (P(None, SLOT, FEAT), P(None, FEAT), P(None, FEAT, SLOT), P())
    return jax.shard_map(local, mesh=split, in_specs=in_specs, out_specs=out_specs, check_vma=False)
```

profile of v0, /device:TPU:32, one launch (start us, length us, event | category | flops | bytes accessed | tf_op | source)
XLA Modules:
  0.0 258.0 jit_solution(12020248933589295281)
XLA Ops:
  7.2 1.4 fusion.26
  8.6 1.4 fusion.28
  9.9 1.4 fusion.30
  11.3 1.3 pad_maximum_fusion.1
  12.6 87.5 %all-reduce.3.cloned.1.call-done = f32[256,1536]{1,0:T(8,128)} async-done(((f32[256,1536]{1,0:T(8,128)}), f32[256,1536]{1,0:T(8,128)}) %all-reduce.3.cloned.1.call-update) | async-done | bytes 1572880 | tf_op jit(solution)/shard_map/psum | solution.py:67
  100.1 1.6 maximum_convert_fusion
  103.4 1.2 copy.15
  104.6 9.8 %all-to-all-start = ((f32[32,8,864]{2,1,0:T(8,128)}), f32[32,8,864]{2,1,0:T(8,128)S(1)}, u32[]{:S(2)}, u32[]{:S(2)}) async-start(f32[32,8,864]{2,1,0:T(8,128)} %bitcast.107), calls=%async_computation | async-start | bytes 1835008 | tf_op jit(solution)/shard_map/all_to_all | solution.py:21
  114.5 2.0 convert_element_type.33
  116.5 2.0 constant_dynamic-slice_fusion
  119.7 22.4 %all-to-all-done = f32[32,8,864]{2,1,0:T(8,128)S(1)} async-done(((f32[32,8,864]{2,1,0:T(8,128)}), f32[32,8,864]{2,1,0:T(8,128)S(1)}, u32[]{:S(2)}, u32[]{:S(2)}) %all-to-all-start) | async-done | bytes 884768 | tf_op jit(solution)/shard_map/all_to_all | solution.py:21
  142.8 21.1 %all_to_all.10 = bf16[32,8,864]{2,1,0:T(8,128)(2,1)S(1)} all-to-all(bf16[32,8,864]{2,1,0:T(8,128)(2,1)S(1)} %broadcast_in_dim.12), channel_id=1, replica_groups=mesh['slot_0'=2,'slot_1'=4,'feat_0'=2,'feat_1'=8,'feat_2'=2] {'feat_0','..., dimensions={0} | all-to-all | bytes 884736 | tf_op jit(solution)/shard_map/all_to_all | solution.py:31
  166.0 1.3 pad_maximum_fusion.2
  167.3 5.6 %psum.51 = f32[]{:T(128)} all-reduce(f32[]{:T(128)} %get-tuple-element.6), channel_id=1, replica_groups=mesh['slot_0'=2,'slot_1'=4,'feat_0'=2,'feat_1'=8,'feat_2'=2] {'slot_0'}, use_global_device_ids=true, to_apply=%region_5.6 | all-reduce | flops 1 | bytes 8 | tf_op jit(solution)/shard_map/psum | solution.py:26
  172.8 9.6 %psum.52 = f32[]{:T(128)} all-reduce(f32[]{:T(128)} %psum.51), channel_id=1, replica_groups=mesh['slot_0'=2,'slot_1'=4,'feat_0'=2,'feat_1'=8,'feat_2'=2] {'slot_1'}, use_global_device_ids=true, to_apply=%region_6.7 | all-reduce | flops 1 | bytes 8 | tf_op jit(solution)/shard_map/psum | solution.py:26
  182.5 7.1 %psum.53 = f32[]{:T(128)} all-reduce(f32[]{:T(128)} %psum.52), channel_id=1, replica_groups=mesh['slot_0'=2,'slot_1'=4,'feat_0'=2,'feat_1'=8,'feat_2'=2] {'feat_0'}, use_global_device_ids=true, to_apply=%region_7.8 | all-reduce | flops 1 | bytes 8 | tf_op jit(solution)/shard_map/psum | solution.py:26
  189.5 15.8 %psum.54 = f32[]{:T(128)} all-reduce(f32[]{:T(128)} %psum.53), channel_id=1, replica_groups=mesh['slot_0'=2,'slot_1'=4,'feat_0'=2,'feat_1'=8,'feat_2'=2] {'feat_1'}, use_global_device_ids=true, to_apply=%region_8.9 | all-reduce | flops 1 | bytes 8 | tf_op jit(solution)/shard_map/psum | solution.py:26
  205.3 3.1 %psum.55 = f32[]{:T(128)} all-reduce(f32[]{:T(128)} %psum.54), channel_id=1, replica_groups=mesh['slot_0'=2,'slot_1'=4,'feat_0'=2,'feat_1'=8,'feat_2'=2] {'feat_2'}, use_global_device_ids=true, to_apply=%region_9.10 | all-reduce | flops 1 | bytes 8 | tf_op jit(solution)/shard_map/psum | solution.py:26
  211.3 1.2 fusion.3
  212.6 1.2 fusion.2
  215.0 1.2 fusion
  216.2 29.3 %all-reduce.5.cloned.1.call-done = f32[256,1536]{1,0:T(8,128)} async-done(((f32[256,1536]{1,0:T(8,128)}), f32[256,1536]{1,0:T(8,128)}) %all-reduce.5.cloned.1.call-update) | async-done | bytes 1572880 | tf_op jit(solution)/shard_map/psum | solution.py:115
  245.5 1.8 fusion.6
  248.6 1.3 pad_maximum_fusion
  (40 shorter events, 10.6 us)
Async XLA Ops:
  7.2 92.9 %all-reduce.3.cloned.1.call-start = ((), (), s32[]{:S(2)}) async-start(), calls=%async_computation.2 | async-start | bytes 3145728 | tf_op jit(solution)/shard_map/psum | solution.py:67
  11.3 1.3 copy-start.3
  12.6 89.1 %copy-start = (bf16[6,512,288]{1,2,0:T(8,128)(2,1)S(1)}, bf16[6,512,288]{1,2,0:T(8,128)(2,1)}, u32[]{:S(2)}) copy-start(bf16[6,512,288]{1,2,0:T(8,128)(2,1)} %param.10) | copy-start | bytes 5308420
  104.6 37.5 %all-to-all-start = ((f32[32,8,864]{2,1,0:T(8,128)}), f32[32,8,864]{2,1,0:T(8,128)S(1)}, u32[]{:S(2)}, u32[]{:S(2)}) async-start(f32[32,8,864]{2,1,0:T(8,128)} %bitcast.107), calls=%async_computation | async-start | bytes 1835008 | tf_op jit(solution)/shard_map/all_to_all | solution.py:21
  114.4 5.2 %copy-start.4 = (f32[3,288]{1,0:T(4,128)S(1)}, f32[3,288]{1,0:T(4,128)}, u32[]{:S(2)}) copy-start(f32[3,288]{1,0:T(4,128)} %param.11) | copy-start | bytes 10372
  114.4 131.1 %all-reduce.5.cloned.1.call-start = ((), (), s32[]{:S(2)}) async-start(), calls=%async_computation.3 | async-start | bytes 3145728 | tf_op jit(solution)/shard_map/psum | solution.py:115
  212.6 33.0 %copy-start.1 = (f32[256,1536]{1,0:T(8,128)S(1)}, f32[256,1536]{1,0:T(8,128)}, u32[]{:S(2)}) copy-start(f32[256,1536]{1,0:T(8,128)} %all-reduce.3.cloned.1.call-done) | copy-start | bytes 4718596
  216.2 31.1 %copy-start.2 = (bf16[3,256,288]{1,2,0:T(8,128)(2,1)S(1)}, bf16[3,256,288]{1,2,0:T(8,128)(2,1)}, u32[]{:S(2)}) copy-start(bf16[3,256,288]{1,2,0:T(8,128)(2,1)} %param.6) | copy-start | bytes 1327108
Sparse Core Ops, SparseCore 0:
  12.7 87.3 all-reduce.2
  167.4 78.1 all-reduce.4
where the time goes:
time: 259 us; the launch traced here: 258 us
  waiting for transfers between devices  139 us (54%)
  blocking collectives  62.2 us (24%)
  between operations  16 us (6%)
  matrix products  15.5 us (6%)
  other arithmetic  9.89 us (4%)
  starting transfers between devices  9.88 us (4%)
  local copies, waits for them, and re-layouts  5.13 us (2%)
    psum x1, waiting for transfers between devices, local(): preact = lax.psum(encode_rows(), SLOT) + bias_row  87.5 us
    psum x5, blocking collectives, over_axes(): return functools.reduce(lax.psum, axes, x)  41.1 us
    psum x1, waiting for transfers between devices, local(): upstream = lax.psum(jnp.concatenate(partials, axis=1), SLOT)  29.3 us
    all_to_all x1, waiting for transfers between devices, sum_at_owner(): lax.all_to_all(tiles, axis, split_axis=0, concat_axis=0, tiled=True)  22.4 us
    all_to_all x1, blocking collectives, sent_to_all(): lax.all_to_all(jnp.broadcast_to(x[None], (devices, *x.shape)), axis, 0, 0...  21.1 us
    all_to_all x1, starting transfers between devices, sum_at_owner(): lax.all_to_all(tiles, axis, split_axis=0, concat_axis=0, tiled=True)  9.8 us
    dot_general x6, matrix products, local(): lax.dot_general(features[:, a * feature_dev:(a + 1) * feature_dev], error...  7.18 us
  transfers between devices with their start and end apart: 3, of which 3 were waited for; matrix products, arithmetic and copies ran while one was open for 5% of the time, Pallas kernels for 0%

commit v1 on v0

--- a/solution.py
+++ b/solution.py
@@ -112,7 +112,7 @@
                 preferred_element_type=jnp.float32,
             )
         partials.append(summed)
-    upstream = lax.psum(jnp.concatenate(partials, axis=1), SLOT)
+    upstream = jnp.sum(lax.all_gather(jnp.concatenate(partials, axis=1), SLOT), axis=0)
     delta = upstream * slopes.astype(jnp.float32)
     bias_grad = jnp.sum(delta, axis=0).reshape(layers, feature_dev)
     delta_half = delta.astype(jnp.bfloat16)

time: 259 us -> 316 us (1.22)
  waiting for transfers between devices: 139 us -> 188 us
  other arithmetic: 9.89 us -> 17.4 us
    all_gather x0 -> x1, waiting for transfers between devices: none -> 78.1 us  [local(): lax.all_gather(jnp.concatenate(partials, axis=1), SLOT)]
    psum x1 -> x0, waiting for transfers between devices: 29.3 us -> none  [local(): upstream = lax.psum(jnp.concatenate(partials, axis=1), SLOT)]
    reduce_sum x0 -> x1, other arithmetic: none -> 7.41 us  [local(): jnp.sum(lax.all_gather(jnp.concatenate(partials, axis=1), SLOT), axis=0)]
  transfers between devices with their start and end apart: 3 -> 3, of which waited for: 3 -> 3; matrix products, arithmetic and copies ran while one was open for 5% -> 4% of each run, Pallas kernels for 0% -> 0%
where the time goes in v1:
time: 316 us; the launch traced here: 315 us
  waiting for transfers between devices  188 us (59%)
  blocking collectives  62.7 us (20%)
  other arithmetic  17.4 us (6%)
  between operations  16.1 us (5%)
  matrix products  15.5 us (5%)
  starting transfers between devices  9.9 us (3%)
  local copies, waits for them, and re-layouts  5.1 us (2%)
    psum x1, waiting for transfers between devices, local(): preact = lax.psum(encode_rows(), SLOT) + bias_row  87.4 us
    all_gather x1, waiting for transfers between devices, local(): lax.all_gather(jnp.concatenate(partials, axis=1), SLOT)  78.1 us
    psum x5, blocking collectives, over_axes(): return functools.reduce(lax.psum, axes, x)  41.6 us
    all_to_all x1, waiting for transfers between devices, sum_at_owner(): lax.all_to_all(tiles, axis, split_axis=0, concat_axis=0, tiled=True)  22.4 us
    all_to_all x1, blocking collectives, sent_to_all(): lax.all_to_all(jnp.broadcast_to(x[None], (devices, *x.shape)), axis, 0, 0...  21.1 us
    all_to_all x1, starting transfers between devices, sum_at_owner(): lax.all_to_all(tiles, axis, split_axis=0, concat_axis=0, tiled=True)  9.82 us
    reduce_sum x1, other arithmetic, local(): jnp.sum(lax.all_gather(jnp.concatenate(partials, axis=1), SLOT), axis=0)  7.41 us
    dot_general x6, matrix products, local(): lax.dot_general(features[:, a * feature_dev:(a + 1) * feature_dev], error...  7.18 us
  transfers between devices with their start and end apart: 3, of which 3 were waited for; matrix products, arithmetic and copies ran while one was open for 4% of the time, Pallas kernels for 0%

profile of v1, /device:TPU:32, one launch (start us, length us, event | category | flops | bytes accessed | tf_op | source)
XLA Modules:
  0.0 314.6 jit_solution(5127203212242815642)
XLA Ops:
  7.2 1.4 fusion.30
  8.6 1.4 fusion.26
  9.9 1.4 fusion.28
  11.3 1.3 pad_maximum_fusion.1
  12.6 87.4 %all-reduce.2.cloned.1.call-done = f32[256,1536]{1,0:T(8,128)} async-done(((f32[256,1536]{1,0:T(8,128)}), f32[256,1536]{1,0:T(8,128)}) %all-reduce.2.cloned.1.call-update) | async-done | bytes 1572880 | tf_op jit(solution)/shard_map/psum | solution.py:67
  100.1 1.6 maximum_convert_fusion
  103.4 1.2 copy.15
  104.6 9.8 %all-to-all-start = ((f32[32,8,864]{2,1,0:T(8,128)}), f32[32,8,864]{2,1,0:T(8,128)S(1)}, u32[]{:S(2)}, u32[]{:S(2)}) async-start(f32[32,8,864]{2,1,0:T(8,128)} %bitcast.109), calls=%async_computation | async-start | bytes 1835008 | tf_op jit(solution)/shard_map/all_to_all | solution.py:21
  114.6 2.0 convert_element_type.33
  116.6 2.0 constant_dynamic-slice_fusion
  119.7 22.4 %all-to-all-done = f32[32,8,864]{2,1,0:T(8,128)S(1)} async-done(((f32[32,8,864]{2,1,0:T(8,128)}), f32[32,8,864]{2,1,0:T(8,128)S(1)}, u32[]{:S(2)}, u32[]{:S(2)}) %all-to-all-start) | async-done | bytes 884768 | tf_op jit(solution)/shard_map/all_to_all | solution.py:21
  142.8 21.1 %all_to_all.10 = bf16[32,8,864]{2,1,0:T(8,128)(2,1)S(1)} all-to-all(bf16[32,8,864]{2,1,0:T(8,128)(2,1)S(1)} %broadcast_in_dim.12), channel_id=1, replica_groups=mesh['slot_0'=2,'slot_1'=4,'feat_0'=2,'feat_1'=8,'feat_2'=2] {'feat_0','..., dimensions={0} | all-to-all | bytes 884736 | tf_op jit(solution)/shard_map/all_to_all | solution.py:31
  166.0 1.3 pad_maximum_fusion.2
  167.2 5.6 %psum.43 = f32[]{:T(128)} all-reduce(f32[]{:T(128)} %get-tuple-element.6), channel_id=1, replica_groups=mesh['slot_0'=2,'slot_1'=4,'feat_0'=2,'feat_1'=8,'feat_2'=2] {'slot_0'}, use_global_device_ids=true, to_apply=%region_5.6 | all-reduce | flops 1 | bytes 8 | tf_op jit(solution)/shard_map/psum | solution.py:26
  172.8 9.7 %psum.44 = f32[]{:T(128)} all-reduce(f32[]{:T(128)} %psum.43), channel_id=1, replica_groups=mesh['slot_0'=2,'slot_1'=4,'feat_0'=2,'feat_1'=8,'feat_2'=2] {'slot_1'}, use_global_device_ids=true, to_apply=%region_6.7 | all-reduce | flops 1 | bytes 8 | tf_op jit(solution)/shard_map/psum | solution.py:26
  182.5 7.4 %psum.45 = f32[]{:T(128)} all-reduce(f32[]{:T(128)} %psum.44), channel_id=1, replica_groups=mesh['slot_0'=2,'slot_1'=4,'feat_0'=2,'feat_1'=8,'feat_2'=2] {'feat_0'}, use_global_device_ids=true, to_apply=%region_7.8 | all-reduce | flops 1 | bytes 8 | tf_op jit(solution)/shard_map/psum | solution.py:26
  189.9 15.8 %psum.46 = f32[]{:T(128)} all-reduce(f32[]{:T(128)} %psum.45), channel_id=1, replica_groups=mesh['slot_0'=2,'slot_1'=4,'feat_0'=2,'feat_1'=8,'feat_2'=2] {'feat_1'}, use_global_device_ids=true, to_apply=%region_8.9 | all-reduce | flops 1 | bytes 8 | tf_op jit(solution)/shard_map/psum | solution.py:26
  205.7 3.1 psum.47
  210.6 1.2 fusion.4
  213.0 1.2 fusion.2
  216.6 78.1 %all-gather.3.cloned.1.call-done = f32[2048,1536]{1,0:T(8,128)} async-done(((f32[256,1536]{1,0:T(8,128)}), f32[2048,1536]{1,0:T(8,128)}) %all-gather.3.cloned.1.call-update) | async-done | bytes 12582928 | tf_op jit(solution)/shard_map/all_gather | solution.py:115
  294.7 7.4 %reduce_sum.37 = f32[256,1536]{1,0:T(8,128)} reduce(f32[8,256,1536]{2,1,0:T(8,128)} %bitcast.108, f32[]{:T(128)} %constant.11.clone.1), dimensions={0}, to_apply=%region_2.3 | reduce | flops 2752512 | bytes 14155780 | tf_op jit(solution)/shard_map/reduce_sum | solution.py:115
  302.1 1.8 fusion.6
  305.3 1.3 pad_maximum_fusion
  (41 shorter events, 11.8 us)
Async XLA Ops:
  7.2 92.9 %all-reduce.2.cloned.1.call-start = ((), (), s32[]{:S(2)}) async-start(), calls=%async_computation.2 | async-start | bytes 3145728 | tf_op jit(solution)/shard_map/psum | solution.py:67
  11.3 1.3 copy-start.3
  12.6 89.1 %copy-start = (bf16[6,512,288]{1,2,0:T(8,128)(2,1)S(1)}, bf16[6,512,288]{1,2,0:T(8,128)(2,1)}, u32[]{:S(2)}) copy-start(bf16[6,512,288]{1,2,0:T(8,128)(2,1)} %param.10) | copy-start | bytes 5308420
  103.3 11.1 %copy-start.4 = (f32[3,288]{1,0:T(4,128)S(1)}, f32[3,288]{1,0:T(4,128)}, u32[]{:S(2)}) copy-start(f32[3,288]{1,0:T(4,128)} %param.11) | copy-start | bytes 10372
  104.6 37.5 %all-to-all-start = ((f32[32,8,864]{2,1,0:T(8,128)}), f32[32,8,864]{2,1,0:T(8,128)S(1)}, u32[]{:S(2)}, u32[]{:S(2)}) async-start(f32[32,8,864]{2,1,0:T(8,128)} %bitcast.109), calls=%async_computation | async-start | bytes 1835008 | tf_op jit(solution)/shard_map/all_to_all | solution.py:21
  114.4 180.3 %all-gather.3.cloned.1.call-start = ((), (), s32[]{:S(2)}) async-start(), calls=%async_computation.3 | async-start | bytes 14155776 | tf_op jit(solution)/shard_map/all_gather | solution.py:115
  294.7 7.4 %copy-start.1 = (f32[256,1536]{1,0:T(8,128)S(1)}, f32[256,1536]{1,0:T(8,128)}, u32[]{:S(2)}) copy-start(f32[256,1536]{1,0:T(8,128)} %all-reduce.2.cloned.1.call-done) | copy-start | bytes 4718596
  302.1 1.8 copy-start.2
Sparse Core Ops, SparseCore 0:
  12.7 87.3 all-reduce.1
  167.4 127.2 all-gather.2
